TPU v7x, 32 devices: a whole 2x2x4 slice. The times are simulated.
32 devices in a mesh: expert: 8 (over z, x), pair: 2 (over core), dp: 2 (over y).
Axes of the slice: x: 2, y: 2, z: 4, core: 2. Of those that a mesh axis runs over, the one named last changes fastest.
Arguments:
- tokens: bfloat16 [128, 196, 768], P(('expert', 'pair', 'dp')), may hold values from -96 to 96
- phi: bfloat16 [768, 16], replicated, may hold values from -0.25 to 0.25
- w_in: bfloat16 [8, 768, 3072], P('expert', None, 'pair'), may hold values from -0.21875 to 0.21875
- w_out: bfloat16 [8, 3072, 768], P('expert', 'pair'), may hold values from -0.109375 to 0.109375
- slot_out: bfloat16 [128, 16, 768], P(('expert', 'pair', 'dp')), may hold values from -6 to 6
- grad_out: bfloat16 [128, 196, 768], P(('expert', 'pair', 'dp')), may hold values from -6 to 6
Outputs:
- token_grad: bfloat16 [128, 196, 768], P(('expert', 'pair', 'dp'))
- phi_grad: float32 [768, 16], replicated
- grad_w_in: bfloat16 [8, 768, 3072], P('expert', 'dp', 'pair')
- grad_w_out: bfloat16 [8, 3072, 768], P('expert', 'pair', 'dp')
All inputs are finite; a program needn't handle non-finite values.
Results may differ from a plain program's by a relative error of at most 0.0086.
Values may be sent and summed in bfloat16 or wider, within the bound.
A program may use at most 128 MiB of HBM per device.

v0:
```python
import jax
import jax.numpy as jnp
from jax import lax
from jax.sharding import PartitionSpec as P


def expert_rows(z_rows, g_rows, w_first, w_second):
    pre = jnp.dot(z_rows, w_first, preferred_element_type=jnp.float32)
    act_full, gelu_back = jax.vjp(jax.nn.gelu, pre)
    act = act_full.astype(jnp.bfloat16)
    dact = lax.dot_general(
        g_rows, w_second, (((1,), (1,)), ((), ())), preferred_element_type=jnp.float32
    )
    dpre = gelu_back(dact)[0].astype(jnp.bfloat16)
    grad_second = lax.dot_general(
        act, g_rows, (((0,), (0,)), ((), ())), preferred_element_type=jnp.float32
    )
    grad_first = lax.dot_general(
        z_rows, dpre, (((0,), (0,)), ((), ())), preferred_element_type=jnp.float32
    )
    back = lax.dot_general(
        dpre, w_first, (((1,), (1,)), ((), ())), preferred_element_type=jnp.float32
    )
    return (grad_first, grad_second, back)


def local(tokens, phi, w_in, w_out, slot_out, grad_out):
    f32 = jnp.float32
    images, _, width = tokens.shape
    groups = lax.axis_size("expert")
    per_group = phi.shape[1] // groups
    experts_here = w_in.shape[0]
    slots = per_group // experts_here
    logits = jnp.einsum("bmd,ds->bms", tokens, phi, preferred_element_type=f32)
    dispatch = jax.nn.softmax(logits, axis=1)
    combine = jax.nn.softmax(logits, axis=2)
    dispatch_low = dispatch.astype(jnp.bfloat16)
    combine_low = combine.astype(jnp.bfloat16)
    slot_in = jnp.einsum("bms,bmd->bsd", dispatch_low, tokens, preferred_element_type=f32).astype(
        jnp.bfloat16
    )
    slot_grad = jnp.einsum(
        "bms,bmd->bsd", combine_low, grad_out, preferred_element_type=f32
    ).astype(jnp.bfloat16)
    outgoing_in = slot_in.reshape(images, groups, per_group, width)
    outgoing_grad = slot_grad.reshape(images, groups, per_group, width)
    arrived_in, arrived_grad = (
        lax.all_to_all(outgoing_in, "expert", split_axis=1, concat_axis=0, tiled=True),
        lax.all_to_all(outgoing_grad, "expert", split_axis=1, concat_axis=0, tiled=True),
    )
    rows_in, rows_grad = (
        lax.all_gather(arrived_in, "pair", axis=0, tiled=True),
        lax.all_gather(arrived_grad, "pair", axis=0, tiled=True),
    )
    count = rows_in.shape[0]
    z_rows = rows_in[:, 0].reshape(count * slots, width)
    g_rows = rows_grad[:, 0].reshape(count * slots, width)
    grad_first, grad_second, back = expert_rows(z_rows, g_rows, w_in[0], w_out[0])
    firsts = [grad_first]
    seconds = [grad_second]
    backs = back.reshape(count, 1, slots, width)
    back_sum = lax.psum_scatter(backs, "pair", scatter_dimension=0, tiled=True)
    grad_w_in = lax.psum_scatter(
        jnp.stack(firsts).astype(jnp.bfloat16), "dp", scatter_dimension=1, tiled=True
    )
    grad_w_out = lax.psum_scatter(
        jnp.stack(seconds).astype(jnp.bfloat16), "dp", scatter_dimension=2, tiled=True
    )
    back_low = back_sum.astype(jnp.bfloat16)
    returned = lax.all_to_all(back_low, "expert", split_axis=0, concat_axis=1, tiled=True)
    slot_in_grad = returned.reshape(images, groups * per_group, width)
    dispatch_grad = jnp.einsum("bmd,bsd->bms", tokens, slot_in_grad, preferred_element_type=f32)
    combine_grad = jnp.einsum("bmd,bsd->bms", grad_out, slot_out, preferred_element_type=f32)
    logit_grad = dispatch * (
        dispatch_grad - jnp.sum(dispatch * dispatch_grad, axis=1, keepdims=True)
    )
    logit_grad = logit_grad + combine * (
        combine_grad - jnp.sum(combine * combine_grad, axis=2, keepdims=True)
    )
    logit_low = logit_grad.astype(jnp.bfloat16)
    token_part = jnp.einsum("bms,bsd->bmd", dispatch_low, slot_in_grad, preferred_element_type=f32)
    token_grad = (
        token_part + jnp.einsum("bms,ds->bmd", logit_low, phi, preferred_element_type=f32)
    ).astype(jnp.bfloat16)
    phi_part = jnp.einsum("bmd,bms->ds", tokens, logit_low, preferred_element_type=f32)
    phi_grad = lax.psum(phi_part, ("expert", "pair", "dp"))
    return (token_grad, phi_grad, grad_w_in, grad_w_out)


def solution(mesh):
    in_specs = (
        P(("expert", "pair", "dp"), None, None),
        P(),
        P("expert", None, "pair"),
        P("expert", "pair", None),
        P(("expert", "pair", "dp"), None, None),
        P(("expert", "pair", "dp"), None, None),
    )
    out_specs = (
        P(("expert", "pair", "dp"), None, None),
        P(),
        P("expert", "dp", "pair"),
        P("expert", "pair", "dp"),
    )
    return jax.shard_map(local, mesh=mesh, in_specs=in_specs, out_specs=out_specs, check_vma=False)
```

profile of v0, /device:TPU:0, one launch (start us, length us, event | category | flops | bytes accessed | tf_op | source)
XLA Modules:
  0.0 153.0 jit_solution(3510893113097627227)
XLA Ops:
  7.2 1.8 %fusion.32 = f32[4,196,16]{1,2,0:T(8,128)S(1)} fusion(bf16[4,196,768]{2,0,1:T(4,128)(2,1)} %param.6, bf16[768,16]{0,1:T(8,128)(2,1)} %param.7), kind=kOutput, calls=%fused_computation.41 | convolution fusion | flops 19267584 | bytes 1278976 | tf_op jit(solution)/shard_map/bmd,ds->bms/dot_general | solution.py:34
  12.1 7.3 %all-to-all-start = ((bf16[4,8,2,768]{3,2,0,1:T(2,128)(2,1)}), bf16[4,8,2,768]{3,2,0,1:T(2,128)(2,1)S(1)}, u32[]{:S(2)}, u32[]{:S(2)}) async-start(bf16[4,8,2,768]{3,2,0,1:T(2,128)(2,1)} %copy.32), calls=%async_computation | async-start | bytes 196608 | tf_op jit(solution)/shard_map/all_to_all | solution.py:49
  22.4 4.0 %all-to-all-done = bf16[4,8,2,768]{3,2,0,1:T(2,128)(2,1)S(1)} async-done(((bf16[4,8,2,768]{3,2,0,1:T(2,128)(2,1)}), bf16[4,8,2,768]{3,2,0,1:T(2,128)(2,1)S(1)}, u32[]{:S(2)}, u32[]{:S(2)}) %all-to-all-start) | async-done | bytes 98336 | tf_op jit(solution)/shard_map/all_to_all | solution.py:49
  26.5 3.4 %all-to-all-start.1 = ((bf16[4,8,2,768]{3,2,0,1:T(2,128)(2,1)}), bf16[4,8,2,768]{3,2,0,1:T(2,128)(2,1)S(1)}, u32[]{:S(2)}, u32[]{:S(2)}) async-start(bf16[4,8,2,768]{3,2,0,1:T(2,128)(2,1)} %copy.35), calls=%async_computation.1 | async-start | bytes 196608 | tf_op jit(solution)/shard_map/all_to_all | solution.py:48
  29.9 1.9 %all_gather.6 = bf16[64,1,2,768]{3,2,1,0:T(2,128)(2,1)S(1)} all-gather(bf16[32,1,2,768]{3,2,1,0:T(2,128)(2,1)S(1)} %bitcast.73), channel_id=1, replica_groups=mesh['expert'=8,'pair'=2,'dp'=2] {'pair'}, dimensions={0}, use_global_device_ids=true | all-gather | bytes 294912 | tf_op jit(solution)/shard_map/all_gather | solution.py:53
  31.9 5.0 %all-to-all-done.1 = bf16[4,8,2,768]{3,2,0,1:T(2,128)(2,1)S(1)} async-done(((bf16[4,8,2,768]{3,2,0,1:T(2,128)(2,1)}), bf16[4,8,2,768]{3,2,0,1:T(2,128)(2,1)S(1)}, u32[]{:S(2)}, u32[]{:S(2)}) %all-to-all-start.1) | async-done | bytes 98336 | tf_op jit(solution)/shard_map/all_to_all | solution.py:48
  36.9 1.9 %all_gather.7 = bf16[64,1,2,768]{3,2,1,0:T(2,128)(2,1)S(1)} all-gather(bf16[32,1,2,768]{3,2,1,0:T(2,128)(2,1)S(1)} %bitcast.74), channel_id=1, replica_groups=mesh['expert'=8,'pair'=2,'dp'=2] {'pair'}, dimensions={0}, use_global_device_ids=true | all-gather | bytes 294912 | tf_op jit(solution)/shard_map/all_gather | solution.py:52
  40.6 1.8 %fusion.40 = bf16[128,1536]{1,0:T(8,128)(2,1)} fusion(f32[128,1536]{1,0:T(8,128)S(1)} %fusion.8, bf16[128,768]{1,0:T(8,128)(2,1)S(1)} %reshape_squeeze.6, bf16[1,1536,768]{2,1,0:T(8,128)(2,1)S(1)} %copy-done.7), kind=kOutput, calls=%fused_computation.49 | convolution fusion | flops 305922048 | bytes 3735552 | tf_op jit(solution)/shard_map/dot_general | solution.py:11
  42.4 1.9 %reshape.35 = bf16[64,2,1536]{2,1,0:T(2,128)(2,1)} reshape(bf16[128,1536]{1,0:T(8,128)(2,1)} %fusion.40) | data formatting | bytes 786432 | tf_op jit(solution)/shard_map/reshape.16
  44.3 2.6 %fusion.12 = f32[64,1,2,768]{3,0,2,1:T(8,128)} fusion(bf16[1,768,1536]{2,1,0:T(8,128)(2,1)S(1)} %copy-done, bf16[64,2,1536]{2,1,0:T(2,128)(2,1)} %reshape.35), kind=kOutput, calls=%fused_computation.17 | convolution fusion | flops 301989888 | bytes 3145728 | tf_op jit(solution)/shard_map/dot_general | solution.py:21
  47.0 2.3 %fusion.5 = bf16[1,1536,768]{2,1,0:T(8,128)(2,1)} fusion(bf16[128,768]{1,0:T(8,128)(2,1)S(1)} %reshape_squeeze.6, f32[128,1536]{1,0:T(8,128)S(1)} %fusion.8), kind=kOutput, calls=%fused_computation.7 | convolution fusion | flops 304939008 | bytes 3342336 | tf_op jit(solution)/shard_map/dot_general | solution.py:15
  49.3 12.2 %copy.44 = bf16[1,1536,768]{1,0,2:T(2,128)(2,1)} copy(bf16[1,1536,768]{2,1,0:T(8,128)(2,1)} %fusion.5) | data formatting | bytes 4718592
  61.5 4.4 %copy.63 = bf16[768,1,1536]{2,0,1:T(8,128)(2,1)} copy(bf16[768,1,1536]{2,1,0:T(2,128)(2,1)} %bitcast.69) | data formatting | bytes 4718592
  66.8 2.2 %fusion.4 = bf16[1,768,1536]{2,1,0:T(8,128)(2,1)} fusion(bf16[128,768]{1,0:T(8,128)(2,1)S(1)} %reshape_squeeze.7, bf16[128,1536]{1,0:T(8,128)(2,1)S(1)} %copy-done.1), kind=kOutput, calls=%fused_computation.6 | convolution fusion | flops 303169536 | bytes 2949120 | tf_op jit(solution)/shard_map/dot_general | solution.py:18
  70.0 1.8 %fusion.25 = f32[4,196,16]{1,2,0:T(8,128)S(1)} fusion(bf16[4,16,768]{2,1,0:T(8,128)(2,1)S(1)} %copy-done.8, bf16[4,196,768]{2,0,1:T(4,128)(2,1)} %param.11), kind=kOutput, calls=%fused_computation.34 | convolution fusion | flops 19267584 | bytes 1352704 | tf_op jit(solution)/shard_map/bmd,bsd->bms/dot_general | solution.py:73
  73.5 3.5 %all-to-all-start.2 = ((bf16[32,1,2,768]{3,2,1,0:T(2,128)(2,1)}), bf16[32,1,2,768]{3,2,1,0:T(2,128)(2,1)S(1)}, u32[]{:S(2)}, u32[]{:S(2)}) async-start(bf16[32,1,2,768]{3,2,1,0:T(2,128)(2,1)} %copy.38), calls=%async_computation.3 | async-start | bytes 196608 | tf_op jit(solution)/shard_map/all_to_all | solution.py:70
  77.3 6.8 %all-to-all-done.2 = bf16[32,1,2,768]{3,2,1,0:T(2,128)(2,1)S(1)} async-done(((bf16[32,1,2,768]{3,2,1,0:T(2,128)(2,1)}), bf16[32,1,2,768]{3,2,1,0:T(2,128)(2,1)S(1)}, u32[]{:S(2)}, u32[]{:S(2)}) %all-to-all-start.2) | async-done | bytes 98336 | tf_op jit(solution)/shard_map/all_to_all | solution.py:70
  86.0 2.2 %fusion.28 = f32[4,196,768]{2,1,0:T(8,128)} fusion(f32[4,196,16]{1,2,0:T(8,128)S(1)} %fusion.23, f32[4,196,16]{1,2,0:T(8,128)S(1)} %convolution_bitcast_fusion, bf16[768,16]{0,1:T(8,128)(2,1)S(1)} %copy-done.6, f32[4,196,16]{1,2,0:T(8,128)S(1)} %copy-done.4, f32[4,16]{1,0:T(4,128)S(1)} %get-tuple-element.18), kind=kOutput, calls=%fused_computation.37 | convolution fusion | flops 19355652 | bytes 2583808 | tf_op jit(solution)/shard_map/bms,ds->bmd/dot_general | solution.py:83
  88.1 3.6 %add_convert_fusion = bf16[4,196,768]{2,1,0:T(8,128)(2,1)} fusion(f32[4,196,768]{2,1,0:T(8,128)} %fusion.28, bf16[4,16,768]{2,1,0:T(8,128)(2,1)S(1)} %reshape.36, f32[4,16]{1,0:T(4,128)S(1)} %get-tuple-element.18, f32[4,196,16]{1,2,0:T(8,128)S(1)} %copy-done.3), kind=kOutput, calls=%fused_computation.8 | convolution fusion | flops 20509700 | bytes 3761408 | tf_op jit(solution)/shard_map/bms,bsd->bmd/dot_general | solution.py:81
  91.7 2.8 %copy.43 = bf16[4,196,768]{2,0,1:T(4,128)(2,1)} copy(bf16[4,196,768]{2,1,0:T(8,128)(2,1)} %add_convert_fusion) | data formatting | bytes 2408448
  94.6 1.7 %convolution_bitcast_fusion.1 = f32[768,16]{0,1:T(8,128)S(1)} fusion(f32[4,196,16]{1,2,0:T(8,128)S(1)} %fusion.23, f32[4,196,16]{1,2,0:T(8,128)S(1)} %convolution_bitcast_fusion, bf16[4,196,768]{2,0,1:T(4,128)(2,1)} %param.6, f32[4,196,16]{1,2,0:T(8,128)S(1)} %copy-done.4, f32[4,16]{1,0:T(4,128)S(1)} %get-tuple-element.18), kind=kOutput, calls=%fused_computation.33 | convolution fusion | flops 19355652 | bytes 1404160 | tf_op jit(solution)/shard_map/bmd,bms->ds/dot_general | solution.py:85
  96.3 39.8 %psum.7 = f32[768,16]{0,1:T(8,128)} all-reduce(f32[768,16]{0,1:T(8,128)S(1)} %convolution_bitcast_fusion.1), channel_id=1, replica_groups=mesh['expert'=8,'pair'=2,'dp'=2] {'expert','pair','dp'}, use_global_device_ids=true, to_apply=%region_7.0 | all-reduce | flops 12288 | bytes 98304 | tf_op jit(solution)/shard_map/psum | solution.py:86
  136.1 3.9 %reshape_bitcast_fusion = bf16[1,1536,384]{1,0,2:T(2,128)(2,1)} fusion(bf16[384,1536]{1,0:T(8,128)(2,1)} %reduce-scatter.10.cloned.1.call-done), kind=kLoop, calls=%fused_computation.10 | loop fusion | bytes 2359296
  140.1 6.4 %copy.45 = bf16[1,1536,384]{2,1,0:T(8,128)(2,1)} copy(bf16[1,1536,384]{1,0,2:T(2,128)(2,1)} %reshape_bitcast_fusion) | data formatting | bytes 2359296
  (44 shorter events, 13.7 us)
Async XLA Ops:
  7.2 31.8 %copy-start = (bf16[1,768,1536]{2,1,0:T(8,128)(2,1)S(1)}, bf16[1,768,1536]{2,1,0:T(8,128)(2,1)}, u32[]{:S(2)}) copy-start(bf16[1,768,1536]{2,1,0:T(8,128)(2,1)} %param.8) | copy-start | bytes 7077892
  9.0 12.7 %copy-start.2 = (f32[4,196,16]{1,2,0:T(8,128)}, f32[4,196,16]{1,2,0:T(8,128)S(1)}, u32[]{:S(2)}) copy-start(f32[4,196,16]{1,2,0:T(8,128)S(1)} %fusion.32) | copy-start | bytes 150532
  12.1 14.4 %all-to-all-start = ((bf16[4,8,2,768]{3,2,0,1:T(2,128)(2,1)}), bf16[4,8,2,768]{3,2,0,1:T(2,128)(2,1)S(1)}, u32[]{:S(2)}, u32[]{:S(2)}) async-start(bf16[4,8,2,768]{3,2,0,1:T(2,128)(2,1)} %copy.32), calls=%async_computation | async-start | bytes 196608 | tf_op jit(solution)/shard_map/all_to_all | solution.py:49
  26.5 10.4 %all-to-all-start.1 = ((bf16[4,8,2,768]{3,2,0,1:T(2,128)(2,1)}), bf16[4,8,2,768]{3,2,0,1:T(2,128)(2,1)S(1)}, u32[]{:S(2)}, u32[]{:S(2)}) async-start(bf16[4,8,2,768]{3,2,0,1:T(2,128)(2,1)} %copy.35), calls=%async_computation.1 | async-start | bytes 196608 | tf_op jit(solution)/shard_map/all_to_all | solution.py:48
  29.8 42.0 %reduce-scatter.6.cloned.1.call-start = ((), (), s32[]{:S(2)}) async-start(), calls=%async_computation.6 | async-start | bytes 589824 | tf_op jit(solution)/shard_map/reduce_scatter | solution.py:62
  38.9 1.7 %copy-start.7 = (bf16[1,1536,768]{2,1,0:T(8,128)(2,1)S(1)}, bf16[1,1536,768]{2,1,0:T(8,128)(2,1)}, u32[]{:S(2)}) copy-start(bf16[1,1536,768]{2,1,0:T(8,128)(2,1)} %param.9) | copy-start | bytes 7077892
  46.9 89.2 %reduce-scatter.10.cloned.1.call-start = ((), (), s32[]{:S(2)}) async-start(), calls=%async_computation.8 | async-start | bytes 3538944
  65.8 1.0 copy-start.1
  65.9 80.6 %reduce-scatter.8.cloned.1.call-start = ((), (), s32[]{:S(2)}) async-start(), calls=%async_computation.7 | async-start | bytes 3538944 | tf_op jit(solution)/shard_map/reduce_scatter | solution.py:63
  69.1 0.9 copy-start.8
  70.0 7.1 %copy-start.5 = (f32[4,196,16]{1,2,0:T(8,128)S(1)}, f32[4,196,16]{1,2,0:T(8,128)}, u32[]{:S(2)}) copy-start(f32[4,196,16]{1,2,0:T(8,128)} %get-tuple-element.17) | copy-start | bytes 150532
  73.5 12.4 %copy-start.4 = (f32[4,196,16]{1,2,0:T(8,128)S(1)}, f32[4,196,16]{1,2,0:T(8,128)}, u32[]{:S(2)}) copy-start(f32[4,196,16]{1,2,0:T(8,128)} %get-tuple-element.19) | copy-start | bytes 150532
  73.5 12.4 %copy-start.6 = (bf16[768,16]{0,1:T(8,128)(2,1)S(1)}, bf16[768,16]{0,1:T(8,128)(2,1)}, u32[]{:S(2)}) copy-start(bf16[768,16]{0,1:T(8,128)(2,1)} %param.7) | copy-start | bytes 73732
  73.5 10.6 %all-to-all-start.2 = ((bf16[32,1,2,768]{3,2,1,0:T(2,128)(2,1)}), bf16[32,1,2,768]{3,2,1,0:T(2,128)(2,1)S(1)}, u32[]{:S(2)}, u32[]{:S(2)}) async-start(bf16[32,1,2,768]{3,2,1,0:T(2,128)(2,1)} %copy.38), calls=%async_computation.3 | async-start | bytes 196608 | tf_op jit(solution)/shard_map/all_to_all | solution.py:70
  85.9 2.2 %copy-start.3 = (f32[4,196,16]{1,2,0:T(8,128)S(1)}, f32[4,196,16]{1,2,0:T(8,128)}, u32[]{:S(2)}) copy-start(f32[4,196,16]{1,2,0:T(8,128)} %copy-done.2) | copy-start | bytes 150532
Sparse Core Ops, SparseCore 0:
  47.1 5.4 reduce-scatter.5
  66.0 32.4 reduce-scatter.9
  101.3 35.5 reduce-scatter.7
where the time goes:
time: 154 us; the launch traced here: 153 us
  blocking collectives  43.7 us (28%)
  local copies, waits for them, and re-layouts  37.2 us (24%)
  matrix products  25.5 us (17%)
  waiting for transfers between devices  15.9 us (10%)
  starting transfers between devices  14.3 us (9%)
  between operations  13.9 us (9%)
  other arithmetic  2.6 us (2%)
    psum x1, blocking collectives, local(): phi_grad = lax.psum(phi_part, ('expert', 'pair', 'dp'))  39.8 us
    unnamed x23, local copies, waits for them, and re-layouts  32.8 us
    all_to_all x1, starting transfers between devices, local(): lax.all_to_all(outgoing_grad, 'expert', split_axis=1, concat_axis=0, tile...  7.28 us
    all_to_all x1, waiting for transfers between devices, local(): lax.all_to_all(back_low, 'expert', split_axis=0, concat_axis=1, tiled=True)  6.84 us
    all_to_all x1, waiting for transfers between devices, local(): lax.all_to_all(outgoing_in, 'expert', split_axis=1, concat_axis=0, tiled=...  4.98 us
    all_to_all x1, waiting for transfers between devices, local(): lax.all_to_all(outgoing_grad, 'expert', split_axis=1, concat_axis=0, tile...  4.02 us
    dot_general x1, matrix products, local(): jnp.einsum('bms,bsd->bmd', dispatch_low, slot_in_grad, preferred_element_...  3.6 us
    all_to_all x1, starting transfers between devices, local(): lax.all_to_all(back_low, 'expert', split_axis=0, concat_axis=1, tiled=True)  3.49 us
  transfers between devices with their start and end apart: 6, of which 3 were waited for; matrix products, arithmetic and copies ran while one was open for 33% of the time, Pallas kernels for 0%

commit v1 on v0

--- a/solution.py
+++ b/solution.py
@@ -83,7 +83,8 @@
         token_part + jnp.einsum("bms,ds->bmd", logit_low, phi, preferred_element_type=f32)
     ).astype(jnp.bfloat16)
     phi_part = jnp.einsum("bmd,bms->ds", tokens, logit_low, preferred_element_type=f32)
-    phi_grad = lax.psum(phi_part, ("expert", "pair", "dp"))
+    one_axis = lax.psum(phi_part, ("pair", "dp"))
+    phi_grad = lax.psum(one_axis, "expert")
     return (token_grad, phi_grad, grad_w_in, grad_w_out)
 
 

time: 154 us -> 163 us (1.058)
  blocking collectives: 43.7 us -> 52.2 us
    psum x1 -> x2, blocking collectives: 39.8 us -> 48.3 us  [the longest x1 35.1 us: local(): phi_grad = lax.psum(one_axis, 'expert')]
  transfers between devices with their start and end apart: 6 -> 6, of which waited for: 3 -> 3; matrix products, arithmetic and copies ran while one was open for 33% -> 31% of each run, Pallas kernels for 0% -> 0%
where the time goes in v1:
time: 163 us; the launch traced here: 161 us
  blocking collectives  52.2 us (32%)
  local copies, waits for them, and re-layouts  37.1 us (23%)
  matrix products  25.5 us (16%)
  waiting for transfers between devices  15.9 us (10%)
  starting transfers between devices  14.3 us (9%)
  between operations  13.9 us (9%)
  other arithmetic  2.6 us (2%)
    psum x1, blocking collectives, local(): phi_grad = lax.psum(one_axis, 'expert')  35.1 us
    unnamed x23, local copies, waits for them, and re-layouts  32.7 us
    psum x1, blocking collectives, local(): one_axis = lax.psum(phi_part, ('pair', 'dp'))  13.2 us
    all_to_all x1, starting transfers between devices, local(): lax.all_to_all(outgoing_grad, 'expert', split_axis=1, concat_axis=0, tile...  7.28 us
    all_to_all x1, waiting for transfers between devices, local(): lax.all_to_all(back_low, 'expert', split_axis=0, concat_axis=1, tiled=True)  6.84 us
    all_to_all x1, waiting for transfers between devices, local(): lax.all_to_all(outgoing_in, 'expert', split_axis=1, concat_axis=0, tiled=...  4.98 us
    all_to_all x1, waiting for transfers between devices, local(): lax.all_to_all(outgoing_grad, 'expert', split_axis=1, concat_axis=0, tile...  4.02 us
    dot_general x1, matrix products, local(): jnp.einsum('bms,bsd->bmd', dispatch_low, slot_in_grad, preferred_element_...  3.6 us
  transfers between devices with their start and end apart: 6, of which 3 were waited for; matrix products, arithmetic and copies ran while one was open for 31% of the time, Pallas kernels for 0%

profile of v1, /device:TPU:0, one launch (start us, length us, event | category | flops | bytes accessed | tf_op | source)
XLA Modules:
  0.0 161.5 jit_solution(3264242103628984754)
XLA Ops:
  7.2 1.8 %fusion.32 = f32[4,196,16]{1,2,0:T(8,128)S(1)} fusion(bf16[4,196,768]{2,0,1:T(4,128)(2,1)} %param.6, bf16[768,16]{0,1:T(8,128)(2,1)} %param.7), kind=kOutput, calls=%fused_computation.41 | convolution fusion | flops 19267584 | bytes 1278976 | tf_op jit(solution)/shard_map/bmd,ds->bms/dot_general | solution.py:34
  12.1 7.3 %all-to-all-start = ((bf16[4,8,2,768]{3,2,0,1:T(2,128)(2,1)}), bf16[4,8,2,768]{3,2,0,1:T(2,128)(2,1)S(1)}, u32[]{:S(2)}, u32[]{:S(2)}) async-start(bf16[4,8,2,768]{3,2,0,1:T(2,128)(2,1)} %copy.32), calls=%async_computation | async-start | bytes 196608 | tf_op jit(solution)/shard_map/all_to_all | solution.py:49
  22.4 4.0 %all-to-all-done = bf16[4,8,2,768]{3,2,0,1:T(2,128)(2,1)S(1)} async-done(((bf16[4,8,2,768]{3,2,0,1:T(2,128)(2,1)}), bf16[4,8,2,768]{3,2,0,1:T(2,128)(2,1)S(1)}, u32[]{:S(2)}, u32[]{:S(2)}) %all-to-all-start) | async-done | bytes 98336 | tf_op jit(solution)/shard_map/all_to_all | solution.py:49
  26.5 3.4 %all-to-all-start.1 = ((bf16[4,8,2,768]{3,2,0,1:T(2,128)(2,1)}), bf16[4,8,2,768]{3,2,0,1:T(2,128)(2,1)S(1)}, u32[]{:S(2)}, u32[]{:S(2)}) async-start(bf16[4,8,2,768]{3,2,0,1:T(2,128)(2,1)} %copy.35), calls=%async_computation.1 | async-start | bytes 196608 | tf_op jit(solution)/shard_map/all_to_all | solution.py:48
  29.9 1.9 %all_gather.6 = bf16[64,1,2,768]{3,2,1,0:T(2,128)(2,1)S(1)} all-gather(bf16[32,1,2,768]{3,2,1,0:T(2,128)(2,1)S(1)} %bitcast.73), channel_id=1, replica_groups=mesh['expert'=8,'pair'=2,'dp'=2] {'pair'}, dimensions={0}, use_global_device_ids=true | all-gather | bytes 294912 | tf_op jit(solution)/shard_map/all_gather | solution.py:53
  31.9 5.0 %all-to-all-done.1 = bf16[4,8,2,768]{3,2,0,1:T(2,128)(2,1)S(1)} async-done(((bf16[4,8,2,768]{3,2,0,1:T(2,128)(2,1)}), bf16[4,8,2,768]{3,2,0,1:T(2,128)(2,1)S(1)}, u32[]{:S(2)}, u32[]{:S(2)}) %all-to-all-start.1) | async-done | bytes 98336 | tf_op jit(solution)/shard_map/all_to_all | solution.py:48
  36.9 1.9 %all_gather.7 = bf16[64,1,2,768]{3,2,1,0:T(2,128)(2,1)S(1)} all-gather(bf16[32,1,2,768]{3,2,1,0:T(2,128)(2,1)S(1)} %bitcast.74), channel_id=1, replica_groups=mesh['expert'=8,'pair'=2,'dp'=2] {'pair'}, dimensions={0}, use_global_device_ids=true | all-gather | bytes 294912 | tf_op jit(solution)/shard_map/all_gather | solution.py:52
  40.6 1.8 %fusion.40 = bf16[128,1536]{1,0:T(8,128)(2,1)} fusion(f32[128,1536]{1,0:T(8,128)S(1)} %fusion.8, bf16[128,768]{1,0:T(8,128)(2,1)S(1)} %reshape_squeeze.6, bf16[1,1536,768]{2,1,0:T(8,128)(2,1)S(1)} %copy-done.7), kind=kOutput, calls=%fused_computation.49 | convolution fusion | flops 305922048 | bytes 3735552 | tf_op jit(solution)/shard_map/dot_general | solution.py:11
  42.4 1.9 %reshape.35 = bf16[64,2,1536]{2,1,0:T(2,128)(2,1)} reshape(bf16[128,1536]{1,0:T(8,128)(2,1)} %fusion.40) | data formatting | bytes 786432 | tf_op jit(solution)/shard_map/reshape.16
  44.3 2.6 %fusion.12 = f32[64,1,2,768]{3,0,2,1:T(8,128)} fusion(bf16[1,768,1536]{2,1,0:T(8,128)(2,1)S(1)} %copy-done, bf16[64,2,1536]{2,1,0:T(2,128)(2,1)} %reshape.35), kind=kOutput, calls=%fused_computation.17 | convolution fusion | flops 301989888 | bytes 3145728 | tf_op jit(solution)/shard_map/dot_general | solution.py:21
  47.0 2.3 %fusion.5 = bf16[1,1536,768]{2,1,0:T(8,128)(2,1)} fusion(bf16[128,768]{1,0:T(8,128)(2,1)S(1)} %reshape_squeeze.6, f32[128,1536]{1,0:T(8,128)S(1)} %fusion.8), kind=kOutput, calls=%fused_computation.7 | convolution fusion | flops 304939008 | bytes 3342336 | tf_op jit(solution)/shard_map/dot_general | solution.py:15
  49.3 12.2 %copy.44 = bf16[1,1536,768]{1,0,2:T(2,128)(2,1)} copy(bf16[1,1536,768]{2,1,0:T(8,128)(2,1)} %fusion.5) | data formatting | bytes 4718592
  61.5 4.4 %copy.63 = bf16[768,1,1536]{2,0,1:T(8,128)(2,1)} copy(bf16[768,1,1536]{2,1,0:T(2,128)(2,1)} %bitcast.69) | data formatting | bytes 4718592
  66.8 2.2 %fusion.4 = bf16[1,768,1536]{2,1,0:T(8,128)(2,1)} fusion(bf16[128,768]{1,0:T(8,128)(2,1)S(1)} %reshape_squeeze.7, bf16[128,1536]{1,0:T(8,128)(2,1)S(1)} %copy-done.1), kind=kOutput, calls=%fused_computation.6 | convolution fusion | flops 303169536 | bytes 2949120 | tf_op jit(solution)/shard_map/dot_general | solution.py:18
  70.0 1.8 %fusion.25 = f32[4,196,16]{1,2,0:T(8,128)S(1)} fusion(bf16[4,16,768]{2,1,0:T(8,128)(2,1)S(1)} %copy-done.8, bf16[4,196,768]{2,0,1:T(4,128)(2,1)} %param.11), kind=kOutput, calls=%fused_computation.34 | convolution fusion | flops 19267584 | bytes 1352704 | tf_op jit(solution)/shard_map/bmd,bsd->bms/dot_general | solution.py:73
  73.5 3.5 %all-to-all-start.2 = ((bf16[32,1,2,768]{3,2,1,0:T(2,128)(2,1)}), bf16[32,1,2,768]{3,2,1,0:T(2,128)(2,1)S(1)}, u32[]{:S(2)}, u32[]{:S(2)}) async-start(bf16[32,1,2,768]{3,2,1,0:T(2,128)(2,1)} %copy.38), calls=%async_computation.3 | async-start | bytes 196608 | tf_op jit(solution)/shard_map/all_to_all | solution.py:70
  77.3 6.8 %all-to-all-done.2 = bf16[32,1,2,768]{3,2,1,0:T(2,128)(2,1)S(1)} async-done(((bf16[32,1,2,768]{3,2,1,0:T(2,128)(2,1)}), bf16[32,1,2,768]{3,2,1,0:T(2,128)(2,1)S(1)}, u32[]{:S(2)}, u32[]{:S(2)}) %all-to-all-start.2) | async-done | bytes 98336 | tf_op jit(solution)/shard_map/all_to_all | solution.py:70
  86.0 2.2 %fusion.28 = f32[4,196,768]{2,1,0:T(8,128)} fusion(f32[4,196,16]{1,2,0:T(8,128)S(1)} %fusion.23, f32[4,196,16]{1,2,0:T(8,128)S(1)} %convolution_bitcast_fusion, bf16[768,16]{0,1:T(8,128)(2,1)S(1)} %copy-done.6, f32[4,196,16]{1,2,0:T(8,128)S(1)} %copy-done.4, f32[4,16]{1,0:T(4,128)S(1)} %get-tuple-element.18), kind=kOutput, calls=%fused_computation.37 | convolution fusion | flops 19355652 | bytes 2583808 | tf_op jit(solution)/shard_map/bms,ds->bmd/dot_general | solution.py:83
  88.1 3.6 %add_convert_fusion = bf16[4,196,768]{2,1,0:T(8,128)(2,1)} fusion(f32[4,196,768]{2,1,0:T(8,128)} %fusion.28, bf16[4,16,768]{2,1,0:T(8,128)(2,1)S(1)} %reshape.36, f32[4,16]{1,0:T(4,128)S(1)} %get-tuple-element.18, f32[4,196,16]{1,2,0:T(8,128)S(1)} %copy-done.3), kind=kOutput, calls=%fused_computation.8 | convolution fusion | flops 20509700 | bytes 3761408 | tf_op jit(solution)/shard_map/bms,bsd->bmd/dot_general | solution.py:81
  91.7 2.8 %copy.43 = bf16[4,196,768]{2,0,1:T(4,128)(2,1)} copy(bf16[4,196,768]{2,1,0:T(8,128)(2,1)} %add_convert_fusion) | data formatting | bytes 2408448
  96.3 13.2 %psum.14 = f32[768,16]{0,1:T(8,128)S(1)} all-reduce(f32[768,16]{0,1:T(8,128)S(1)} %convolution_bitcast_fusion.1), channel_id=1, replica_groups=mesh['expert'=8,'pair'=2,'dp'=2] {'pair','dp'}, use_global_device_ids=true, to_apply=%region_7.0 | all-reduce | flops 12288 | bytes 98304 | tf_op jit(solution)/shard_map/psum | solution.py:86
  109.5 35.1 %psum.15 = f32[768,16]{0,1:T(8,128)} all-reduce(f32[768,16]{0,1:T(8,128)S(1)} %psum.14), channel_id=1, replica_groups=mesh['expert'=8,'pair'=2,'dp'=2] {'expert'}, use_global_device_ids=true, to_apply=%region_8.0 | all-reduce | flops 12288 | bytes 98304 | tf_op jit(solution)/shard_map/psum | solution.py:87
  144.6 3.9 %reshape_bitcast_fusion = bf16[1,1536,384]{1,0,2:T(2,128)(2,1)} fusion(bf16[384,1536]{1,0:T(8,128)(2,1)} %reduce-scatter.10.cloned.1.call-done), kind=kLoop, calls=%fused_computation.10 | loop fusion | bytes 2359296
  148.5 6.4 %copy.45 = bf16[1,1536,384]{2,1,0:T(8,128)(2,1)} copy(bf16[1,1536,384]{1,0,2:T(2,128)(2,1)} %reshape_bitcast_fusion) | data formatting | bytes 2359296
  (45 shorter events, 15.5 us)
Async XLA Ops:
  7.2 31.8 %copy-start = (bf16[1,768,1536]{2,1,0:T(8,128)(2,1)S(1)}, bf16[1,768,1536]{2,1,0:T(8,128)(2,1)}, u32[]{:S(2)}) copy-start(bf16[1,768,1536]{2,1,0:T(8,128)(2,1)} %param.8) | copy-start | bytes 7077892
  9.0 12.7 %copy-start.2 = (f32[4,196,16]{1,2,0:T(8,128)}, f32[4,196,16]{1,2,0:T(8,128)S(1)}, u32[]{:S(2)}) copy-start(f32[4,196,16]{1,2,0:T(8,128)S(1)} %fusion.32) | copy-start | bytes 150532
  12.1 14.4 %all-to-all-start = ((bf16[4,8,2,768]{3,2,0,1:T(2,128)(2,1)}), bf16[4,8,2,768]{3,2,0,1:T(2,128)(2,1)S(1)}, u32[]{:S(2)}, u32[]{:S(2)}) async-start(bf16[4,8,2,768]{3,2,0,1:T(2,128)(2,1)} %copy.32), calls=%async_computation | async-start | bytes 196608 | tf_op jit(solution)/shard_map/all_to_all | solution.py:49
  26.5 10.4 %all-to-all-start.1 = ((bf16[4,8,2,768]{3,2,0,1:T(2,128)(2,1)}), bf16[4,8,2,768]{3,2,0,1:T(2,128)(2,1)S(1)}, u32[]{:S(2)}, u32[]{:S(2)}) async-start(bf16[4,8,2,768]{3,2,0,1:T(2,128)(2,1)} %copy.35), calls=%async_computation.1 | async-start | bytes 196608 | tf_op jit(solution)/shard_map/all_to_all | solution.py:48
  29.8 42.0 %reduce-scatter.6.cloned.1.call-start = ((), (), s32[]{:S(2)}) async-start(), calls=%async_computation.6 | async-start | bytes 589824 | tf_op jit(solution)/shard_map/reduce_scatter | solution.py:62
  38.9 1.7 %copy-start.7 = (bf16[1,1536,768]{2,1,0:T(8,128)(2,1)S(1)}, bf16[1,1536,768]{2,1,0:T(8,128)(2,1)}, u32[]{:S(2)}) copy-start(bf16[1,1536,768]{2,1,0:T(8,128)(2,1)} %param.9) | copy-start | bytes 7077892
  46.9 97.7 %reduce-scatter.10.cloned.1.call-start = ((), (), s32[]{:S(2)}) async-start(), calls=%async_computation.8 | async-start | bytes 3538944
  65.8 1.0 copy-start.1
  65.9 89.1 %reduce-scatter.8.cloned.1.call-start = ((), (), s32[]{:S(2)}) async-start(), calls=%async_computation.7 | async-start | bytes 3538944 | tf_op jit(solution)/shard_map/reduce_scatter | solution.py:63
  69.1 0.9 copy-start.8
  70.0 7.1 %copy-start.5 = (f32[4,196,16]{1,2,0:T(8,128)S(1)}, f32[4,196,16]{1,2,0:T(8,128)}, u32[]{:S(2)}) copy-start(f32[4,196,16]{1,2,0:T(8,128)} %get-tuple-element.17) | copy-start | bytes 150532
  73.5 12.4 %copy-start.4 = (f32[4,196,16]{1,2,0:T(8,128)S(1)}, f32[4,196,16]{1,2,0:T(8,128)}, u32[]{:S(2)}) copy-start(f32[4,196,16]{1,2,0:T(8,128)} %get-tuple-element.19) | copy-start | bytes 150532
  73.5 12.4 %copy-start.6 = (bf16[768,16]{0,1:T(8,128)(2,1)S(1)}, bf16[768,16]{0,1:T(8,128)(2,1)}, u32[]{:S(2)}) copy-start(bf16[768,16]{0,1:T(8,128)(2,1)} %param.7) | copy-start | bytes 73732
  73.5 10.6 %all-to-all-start.2 = ((bf16[32,1,2,768]{3,2,1,0:T(2,128)(2,1)}), bf16[32,1,2,768]{3,2,1,0:T(2,128)(2,1)S(1)}, u32[]{:S(2)}, u32[]{:S(2)}) async-start(bf16[32,1,2,768]{3,2,1,0:T(2,128)(2,1)} %copy.38), calls=%async_computation.3 | async-start | bytes 196608 | tf_op jit(solution)/shard_map/all_to_all | solution.py:70
  85.9 2.2 %copy-start.3 = (f32[4,196,16]{1,2,0:T(8,128)S(1)}, f32[4,196,16]{1,2,0:T(8,128)}, u32[]{:S(2)}) copy-start(f32[4,196,16]{1,2,0:T(8,128)} %copy-done.2) | copy-start | bytes 150532
Sparse Core Ops, SparseCore 0:
  47.1 5.4 reduce-scatter.5
  66.0 32.4 reduce-scatter.9
  101.3 34.9 reduce-scatter.7
